TPU v7x, 512 devices: a whole 4x4x16 slice. The times are simulated.
512 devices in a mesh: slab: 128 (over x, z, y_hi), col: 4 (over y_lo, core).
Axes of the slice: x: 4, y: 4 (y_hi: 2, y_lo: 2; y = y_hi * 2 + y_lo), z: 16, core: 2. Of those that a mesh axis runs over, the one named last changes fastest.
Arguments:
- rhs: float32 [1024, 32, 384], P(('slab', 'col')), may hold values from -6 to 6
- tiles: bfloat16 [1024, 6, 384, 384], P(('slab', 'col'))
- neighbours: int32 [1024, 6], P(('slab', 'col')), may hold values from 0 to 1023, as said below
- smoother: bfloat16 [1024, 384, 384], P(('slab', 'col'))
- basis: bfloat16 [1024, 256, 384], P(('slab', 'col')), may hold values from -0.29882812 to 0.29882812
Outputs:
- solution: float32 [1024, 32, 384], P(('slab', 'col'))
- coarse_iterate: float32 [1024, 32, 256], P(('slab', 'col'))
Inputs may be any that keep to these rules, and one draw needn't show every extreme that they name: `neighbours`: entry [g, 0] is g itself; every other entry names a cell whose slab (cell // 8) is the slab of g or one of the two beside it, counted around 128 slabs.
All inputs are finite; a program needn't handle non-finite values.
Results may differ from a plain program's by a relative error of at most 0.0023.
The roundings to bfloat16 on the way count: a program that leaves them out, or rounds other values in their place, can miss the bound.
Values may be sent and summed in bfloat16 or wider, within the bound.
No kernel may reach another device: no remote copies, remote signals or barrier semaphores. Data moves between devices by JAX's collectives and lax.ppermute only.
A program may use at most 128 MiB of HBM per device.

v0:
```python
import jax
import jax.numpy as jnp
from jax import lax
from jax.sharding import PartitionSpec as P

damping = 0.8


def with_halo(cells, sides, width):
    for axis, dim in sides:
        count = lax.axis_size(axis)
        head = lax.slice_in_dim(cells, 0, width, axis=dim)
        tail = lax.slice_in_dim(cells, cells.shape[dim] - width, cells.shape[dim], axis=dim)
        cells = jnp.concatenate(
            [
                lax.ppermute(tail, axis, [(i, (i + 1) % count) for i in range(count)]),
                cells,
                lax.ppermute(head, axis, [((i + 1) % count, i) for i in range(count)]),
            ],
            axis=dim,
        )
    return cells


def neighbour_rows(vec_rounded):
    slab_rows = lax.all_gather(vec_rounded, "col", axis=0, tiled=True)
    return with_halo(slab_rows, (("slab", 0),), slab_rows.shape[0])


def per_device(rhs, tiles, neighbours, smoother, basis):
    cell_dev = rhs.shape[0]
    slab_count = lax.axis_size("slab")
    slab_cells = cell_dev * lax.axis_size("col")
    here = lax.axis_index("slab")
    slab_step = (neighbours // slab_cells - here + 1 + slab_count) % slab_count
    offset = neighbours % slab_cells
    row_place = slab_step * slab_cells + offset

    def smooth(residue):
        return jnp.einsum(
            "gri,gio->gro",
            residue.astype(jnp.bfloat16),
            smoother,
            preferred_element_type=jnp.float32,
        )

    def fine_apply(vec):
        near = neighbour_rows(vec.astype(jnp.bfloat16))
        picked = jnp.take(near, row_place, axis=0)
        return jnp.einsum("gtri,gtio->gro", picked, tiles, preferred_element_type=jnp.float32)

    x_first = smooth(rhs)
    x_second = x_first + smooth(rhs - fine_apply(x_first))
    fine_residual = rhs - fine_apply(x_second)
    wide_basis = lax.all_gather(basis, "col", axis=0, tiled=True)
    near_basis = with_halo(wide_basis, (("slab", 0),), wide_basis.shape[0])
    picked_basis = jnp.take(near_basis, row_place, axis=0)
    upper = jnp.einsum(
        "gtci,gtio->gtco", picked_basis, tiles, preferred_element_type=jnp.float32
    ).astype(jnp.bfloat16)
    coarse_tiles = jnp.einsum(
        "gtco,gdo->gtcd", upper, basis, preferred_element_type=jnp.float32
    ).astype(jnp.bfloat16)
    pivots = jnp.diagonal(coarse_tiles[:, 0].astype(jnp.float32), axis1=1, axis2=2)
    coarse_rhs = jnp.einsum(
        "gri,gci->grc",
        fine_residual.astype(jnp.bfloat16),
        basis,
        preferred_element_type=jnp.float32,
    )
    c_first = damping * coarse_rhs / pivots[:, None, :]
    near_coarse = neighbour_rows(c_first.astype(jnp.bfloat16))
    picked_coarse = jnp.take(near_coarse, row_place, axis=0)
    coarse_image = jnp.einsum(
        "gtrc,gtcd->grd", picked_coarse, coarse_tiles, preferred_element_type=jnp.float32
    )
    coarse_iterate = c_first + damping * (coarse_rhs - coarse_image) / pivots[:, None, :]
    solution = x_second + jnp.einsum(
        "grc,gci->gri",
        coarse_iterate.astype(jnp.bfloat16),
        basis,
        preferred_element_type=jnp.float32,
    )
    return (solution, coarse_iterate)


def solution(mesh):
    placed = (
        P(("slab", "col"), None, None),
        P(("slab", "col"), None, None, None),
        P(("slab", "col"), None),
        P(("slab", "col"), None, None),
        P(("slab", "col"), None, None),
    )
    return jax.shard_map(
        per_device,
        mesh=mesh,
        in_specs=placed,
        out_specs=(P(("slab", "col"), None, None), P(("slab", "col"), None, None)),
        check_vma=False,
    )
```

profile of v0, /device:TPU:1, one launch (start us, length us, event | category | flops | bytes accessed | tf_op | source)
XLA Modules:
  0.0 257.2 jit_solution(5884026762105295184)
XLA Ops:
  7.2 0.0 copy-start
  7.2 0.0 all-gather.2.cloned.1.call-start
  7.2 0.7 all-gather.2.cloned.1.call-update
  7.9 40.4 %all-gather.2.cloned.1.call-done = bf16[8,256,384]{2,1,0:T(8,128)(2,1)} async-done(((bf16[2,256,384]{2,1,0:T(8,128)(2,1)}), bf16[8,256,384]{2,1,0:T(8,128)(2,1)}) %all-gather.2.cloned.1.call-update) | async-done | bytes 1572880 | tf_op jit(solution)/shard_map/all_gather | solution.py:55
  48.3 9.9 %collective-permute-start.5 = (bf16[8,256,384]{2,1,0:T(8,128)(2,1)}, bf16[8,256,384]{2,1,0:T(8,128)(2,1)}, u32[]{:S(2)}, u32[]{:S(2)}) collective-permute-start(bf16[8,256,384]{2,1,0:T(8,128)(2,1)} %all-gather.2.cloned.1.call-done), channel_id=1, source_target_pairs={{4,0},{8,4},{12,8},{16,12},{20,16},{24,20},{28,24},{32,28},{36,32}... | collective-permute-start | bytes 4718600 | tf_op jit(solution)/shard_map/ppermute | solution.py:18
  58.2 1.9 collective-permute-start.4
  60.2 2.0 fusion.56
  62.1 62.8 %all_gather.12 = bf16[8,32,384]{2,1,0:T(8,128)(2,1)} all-gather(bf16[2,32,384]{2,1,0:T(8,128)(2,1)S(1)} %get-tuple-element.5), channel_id=1, replica_groups=mesh['slab'=128,'col'=4] {'col'}, dimensions={0}, use_global_device_ids=true | all-gather | bytes 245760 | tf_op jit(solution)/shard_map/all_gather | solution.py:26
  124.9 8.1 %collective-permute-start.1 = (bf16[8,32,384]{2,1,0:T(8,128)(2,1)}, bf16[8,32,384]{2,1,0:T(8,128)(2,1)}, u32[]{:S(2)}, u32[]{:S(2)}) collective-permute-start(bf16[8,32,384]{2,1,0:T(8,128)(2,1)} %all_gather.12), channel_id=1, source_target_pairs={{4,0},{8,4},{12,8},{16,12},{20,16},{24,20},{28,24},{32,28},{36,32}... | collective-permute-start | bytes 589832 | tf_op jit(solution)/shard_map/ppermute | solution.py:18
  132.9 1.9 collective-permute-start
  134.9 0.7 compare_and_fusion
  135.6 0.1 reshape.64
  135.7 1.7 collective-permute-done.1
  137.3 9.6 %collective-permute-done = bf16[8,32,384]{2,1,0:T(8,128)(2,1)} collective-permute-done((bf16[8,32,384]{2,1,0:T(8,128)(2,1)}, bf16[8,32,384]{2,1,0:T(8,128)(2,1)}, u32[]{:S(2)}, u32[]{:S(2)}) %collective-permute-start) | collective-permute-done | bytes 196640 | tf_op jit(solution)/shard_map/ppermute | solution.py:16
  146.9 2.0 pad_maximum_fusion.1
  148.9 2.4 gather_fusion.3
  151.3 0.0 copy-done
  151.3 2.7 %fusion.57 = (bf16[2,32,384]{2,1,0:T(8,128)(2,1)}, f32[2,32,384]{2,1,0:T(8,128)}) fusion(f32[2,32,384]{2,1,0:T(8,128)} %get-tuple-element.6, bf16[2,384,384]{2,1,0:T(8,128)(2,1)} %param.10, f32[2,32,384]{2,1,0:T(8,128)} %param.7, bf16[2,6,384,384]{3,2,1,0:T(8,128)(2,1)S(1)} %copy-done, bf16[2,6,32,384]{3,2,1,0:T(8,128)(2,1)} %bitcast.60, ...), kind=kOutput, calls=%fused_computation.67 | convolution fusion | flops 132366336 | bytes 4767756 | tf_op jit(solution)/shard_map/gri,gio->gro/dot_general | solution.py:40
  154.0 6.9 %all_gather.13 = bf16[8,32,384]{2,1,0:T(8,128)(2,1)S(1)} all-gather(bf16[2,32,384]{2,1,0:T(8,128)(2,1)} %get-tuple-element.7), channel_id=1, replica_groups=mesh['slab'=128,'col'=4] {'col'}, dimensions={0}, use_global_device_ids=true | all-gather | bytes 245760 | tf_op jit(solution)/shard_map/all_gather | solution.py:26
  160.9 4.2 %collective-permute-start.3 = (bf16[8,32,384]{2,1,0:T(8,128)(2,1)S(1)}, bf16[8,32,384]{2,1,0:T(8,128)(2,1)S(1)}, u32[]{:S(2)}, u32[]{:S(2)}) collective-permute-start(bf16[8,32,384]{2,1,0:T(8,128)(2,1)S(1)} %all_gather.13), channel_id=1, source_target_pairs={{4,0},{8,4},{12,8},{16,12},{20,16},{24,20},{28,24},{32,28},{36,32}... | collective-permute-start | bytes 589832 | tf_op jit(solution)/shard_map/ppermute | solution.py:18
  165.1 2.6 %collective-permute-start.2 = (bf16[8,32,384]{2,1,0:T(8,128)(2,1)S(1)}, bf16[8,32,384]{2,1,0:T(8,128)(2,1)S(1)}, u32[]{:S(2)}, u32[]{:S(2)}) collective-permute-start(bf16[8,32,384]{2,1,0:T(8,128)(2,1)S(1)} %all_gather.13), channel_id=1, source_target_pairs={{0,4},{4,8},{8,12},{12,16},{16,20},{20,24},{24,28},{28,32},{32,36}... | collective-permute-start | bytes 589832 | tf_op jit(solution)/shard_map/ppermute | solution.py:16
  167.7 2.9 %collective-permute-done.3 = bf16[8,32,384]{2,1,0:T(8,128)(2,1)S(1)} collective-permute-done((bf16[8,32,384]{2,1,0:T(8,128)(2,1)S(1)}, bf16[8,32,384]{2,1,0:T(8,128)(2,1)S(1)}, u32[]{:S(2)}, u32[]{:S(2)}) %collective-permute-start.3) | collective-permute-done | bytes 196640 | tf_op jit(solution)/shard_map/ppermute | solution.py:18
  170.6 8.2 %collective-permute-done.2 = bf16[8,32,384]{2,1,0:T(8,128)(2,1)S(1)} collective-permute-done((bf16[8,32,384]{2,1,0:T(8,128)(2,1)S(1)}, bf16[8,32,384]{2,1,0:T(8,128)(2,1)S(1)}, u32[]{:S(2)}, u32[]{:S(2)}) %collective-permute-start.2) | collective-permute-done | bytes 196640 | tf_op jit(solution)/shard_map/ppermute | solution.py:16
  178.8 0.9 pad_maximum_fusion.2
  179.6 2.4 gather_fusion.4
  182.0 0.0 collective-permute-done.5
  182.0 0.0 collective-permute-done.4
  182.0 4.2 %pad_maximum_fusion = bf16[24,256,384]{2,1,0:T(8,128)(2,1)} fusion(bf16[8,256,384]{2,1,0:T(8,128)(2,1)} %collective-permute-done.5, bf16[8,256,384]{2,1,0:T(8,128)(2,1)} %all-gather.2.cloned.1.call-done, bf16[8,256,384]{2,1,0:T(8,128)(2,1)} %collective-permute-done.4), kind=kLoop, calls=%fused_computation.5 | loop fusion | flops 4718592 | bytes 9437184 | tf_op jit(solution)/shard_map/concatenate | solution.py:14
  186.2 4.8 %gather_fusion = bf16[12,256,384]{2,1,0:T(8,128)(2,1)} fusion(bf16[24,256,384]{2,1,0:T(8,128)(2,1)} %pad_maximum_fusion, s32[1024]{0:T(1024)S(1)} %pad_clamp_fusion), kind=kCustom, calls=%fused_computation.2 | custom fusion | bytes 4718640 | tf_op jit(solution)/shard_map/jit(_take)/gather | solution.py:57
  191.0 5.3 %fusion.9 = bf16[2,6,256,256]{3,2,1,0:T(8,128)(2,1)} fusion(bf16[2,6,384,384]{3,2,1,0:T(8,128)(2,1)S(1)} %copy-done, bf16[2,6,256,384]{3,2,1,0:T(8,128)(2,1)} %bitcast.58, pred[2,6]{1,0:T(4,128)(4,1)S(1)} %get-tuple-element.3, bf16[2,256,384]{2,1,0:T(8,128)(2,1)} %param.11), kind=kOutput, calls=%fused_computation.11 | convolution fusion | flops 1513095168 | bytes 7864332 | tf_op jit(solution)/shard_map/gtco,gdo->gtcd/dot_general | solution.py:61
  196.3 1.8 fusion.34
  198.1 17.5 %copy.11 = f32[2,256,256]{0,2,1:T(8,128)} copy(f32[2,256,256]{2,1,0:T(8,128)} %fusion.34) | data formatting | bytes 1048576 | tf_op jit(solution)/shard_map/convert_element_type | solution.py:64
  215.6 3.0 %gather_fusion.1 = f32[256,2]{1,0:T(8,128)} fusion(f32[2,256,256]{0,2,1:T(8,128)} %copy.11, s32[256]{0:T(256)S(1)} %bitcast.57), kind=kCustom, calls=%fused_computation.3 | custom fusion | bytes 6144 | tf_op jit(solution)/shard_map/jit(diagonal)/gather | solution.py:64
  218.5 1.0 copy.12
  219.5 2.6 %fusion.42 = (bf16[2,32,256]{2,1,0:T(8,128)(2,1)}, f32[2,32,256]{2,1,0:T(8,128)}) fusion(f32[2,256]{1,0:T(2,128)S(1)} %copy.12, bf16[2,256,384]{2,1,0:T(8,128)(2,1)} %param.11, f32[2,32,384]{2,1,0:T(8,128)} %param.7, bf16[2,6,384,384]{3,2,1,0:T(8,128)(2,1)S(1)} %copy-done, bf16[2,6,32,384]{3,2,1,0:T(8,128)(2,1)} %bitcast.59, ...), kind=kOutput, calls=%fused_computation.43 | convolution fusion | flops 126074880 | bytes 4425740 | tf_op jit(solution)/shard_map/gri,gci->grc/dot_general | solution.py:65
  222.1 6.7 %all_gather.15 = bf16[8,32,256]{2,1,0:T(8,128)(2,1)S(1)} all-gather(bf16[2,32,256]{2,1,0:T(8,128)(2,1)} %get-tuple-element.9), channel_id=1, replica_groups=mesh['slab'=128,'col'=4] {'col'}, dimensions={0}, use_global_device_ids=true | all-gather | bytes 163840 | tf_op jit(solution)/shard_map/all_gather | solution.py:26
  228.9 2.5 collective-permute-start.7
  231.4 4.3 %collective-permute-start.6 = (bf16[8,32,256]{2,1,0:T(8,128)(2,1)S(1)}, bf16[8,32,256]{2,1,0:T(8,128)(2,1)S(1)}, u32[]{:S(2)}, u32[]{:S(2)}) collective-permute-start(bf16[8,32,256]{2,1,0:T(8,128)(2,1)S(1)} %all_gather.15), channel_id=1, source_target_pairs={{0,4},{4,8},{8,12},{12,16},{16,20},{20,24},{24,28},{28,32},{32,36}... | collective-permute-start | bytes 393224 | tf_op jit(solution)/shard_map/ppermute | solution.py:16
  235.7 1.5 collective-permute-done.7
  237.2 6.4 %collective-permute-done.6 = bf16[8,32,256]{2,1,0:T(8,128)(2,1)S(1)} collective-permute-done((bf16[8,32,256]{2,1,0:T(8,128)(2,1)S(1)}, bf16[8,32,256]{2,1,0:T(8,128)(2,1)S(1)}, u32[]{:S(2)}, u32[]{:S(2)}) %collective-permute-start.6) | collective-permute-done | bytes 131104 | tf_op jit(solution)/shard_map/ppermute | solution.py:16
  243.6 0.8 pad_maximum_fusion.3
  244.4 2.2 gather_fusion.2
  246.6 1.8 fusion.23
  248.4 0.0 copy-start.1
  248.5 1.9 convolution_add_fusion.1
  250.3 0.0 copy-done.1
  (2 shorter events, 0.0 us)
Async XLA Ops:
  7.2 144.1 %copy-start = (bf16[2,6,384,384]{3,2,1,0:T(8,128)(2,1)S(1)}, bf16[2,6,384,384]{3,2,1,0:T(8,128)(2,1)}, u32[]{:S(2)}) copy-start(bf16[2,6,384,384]{3,2,1,0:T(8,128)(2,1)} %param.8) | copy-start | bytes 10616836
  7.2 41.1 %all-gather.2.cloned.1.call-start = ((), (), s32[]{:S(2)}) async-start(), calls=%async_computation | async-start | bytes 1966080 | tf_op jit(solution)/shard_map/all_gather | solution.py:55
  48.3 133.8 %collective-permute-start.5 = (bf16[8,256,384]{2,1,0:T(8,128)(2,1)}, bf16[8,256,384]{2,1,0:T(8,128)(2,1)}, u32[]{:S(2)}, u32[]{:S(2)}) collective-permute-start(bf16[8,256,384]{2,1,0:T(8,128)(2,1)} %all-gather.2.cloned.1.call-done), channel_id=1, source_target_pairs={{4,0},{8,4},{12,8},{16,12},{20,16},{24,20},{28,24},{32,28},{36,32}... | collective-permute-start | bytes 4718600 | tf_op jit(solution)/shard_map/ppermute | solution.py:18
  58.2 123.8 %collective-permute-start.4 = (bf16[8,256,384]{2,1,0:T(8,128)(2,1)}, bf16[8,256,384]{2,1,0:T(8,128)(2,1)}, u32[]{:S(2)}, u32[]{:S(2)}) collective-permute-start(bf16[8,256,384]{2,1,0:T(8,128)(2,1)} %all-gather.2.cloned.1.call-done), channel_id=1, source_target_pairs={{0,4},{4,8},{8,12},{12,16},{16,20},{20,24},{24,28},{28,32},{32,36}... | collective-permute-start | bytes 4718600 | tf_op jit(solution)/shard_map/ppermute | solution.py:16
  124.9 12.5 %collective-permute-start.1 = (bf16[8,32,384]{2,1,0:T(8,128)(2,1)}, bf16[8,32,384]{2,1,0:T(8,128)(2,1)}, u32[]{:S(2)}, u32[]{:S(2)}) collective-permute-start(bf16[8,32,384]{2,1,0:T(8,128)(2,1)} %all_gather.12), channel_id=1, source_target_pairs={{4,0},{8,4},{12,8},{16,12},{20,16},{24,20},{28,24},{32,28},{36,32}... | collective-permute-start | bytes 589832 | tf_op jit(solution)/shard_map/ppermute | solution.py:18
  132.9 14.0 %collective-permute-start = (bf16[8,32,384]{2,1,0:T(8,128)(2,1)}, bf16[8,32,384]{2,1,0:T(8,128)(2,1)}, u32[]{:S(2)}, u32[]{:S(2)}) collective-permute-start(bf16[8,32,384]{2,1,0:T(8,128)(2,1)} %all_gather.12), channel_id=1, source_target_pairs={{0,4},{4,8},{8,12},{12,16},{16,20},{20,24},{24,28},{28,32},{32,36}... | collective-permute-start | bytes 589832 | tf_op jit(solution)/shard_map/ppermute | solution.py:16
  160.9 9.7 %collective-permute-start.3 = (bf16[8,32,384]{2,1,0:T(8,128)(2,1)S(1)}, bf16[8,32,384]{2,1,0:T(8,128)(2,1)S(1)}, u32[]{:S(2)}, u32[]{:S(2)}) collective-permute-start(bf16[8,32,384]{2,1,0:T(8,128)(2,1)S(1)} %all_gather.13), channel_id=1, source_target_pairs={{4,0},{8,4},{12,8},{16,12},{20,16},{24,20},{28,24},{32,28},{36,32}... | collective-permute-start | bytes 589832 | tf_op jit(solution)/shard_map/ppermute | solution.py:18
  165.1 13.6 %collective-permute-start.2 = (bf16[8,32,384]{2,1,0:T(8,128)(2,1)S(1)}, bf16[8,32,384]{2,1,0:T(8,128)(2,1)S(1)}, u32[]{:S(2)}, u32[]{:S(2)}) collective-permute-start(bf16[8,32,384]{2,1,0:T(8,128)(2,1)S(1)} %all_gather.13), channel_id=1, source_target_pairs={{0,4},{4,8},{8,12},{12,16},{16,20},{20,24},{24,28},{28,32},{32,36}... | collective-permute-start | bytes 589832 | tf_op jit(solution)/shard_map/ppermute | solution.py:16
  228.9 8.3 %collective-permute-start.7 = (bf16[8,32,256]{2,1,0:T(8,128)(2,1)S(1)}, bf16[8,32,256]{2,1,0:T(8,128)(2,1)S(1)}, u32[]{:S(2)}, u32[]{:S(2)}) collective-permute-start(bf16[8,32,256]{2,1,0:T(8,128)(2,1)S(1)} %all_gather.15), channel_id=1, source_target_pairs={{4,0},{8,4},{12,8},{16,12},{20,16},{24,20},{28,24},{32,28},{36,32}... | collective-permute-start | bytes 393224 | tf_op jit(solution)/shard_map/ppermute | solution.py:18
  231.4 12.2 %collective-permute-start.6 = (bf16[8,32,256]{2,1,0:T(8,128)(2,1)S(1)}, bf16[8,32,256]{2,1,0:T(8,128)(2,1)S(1)}, u32[]{:S(2)}, u32[]{:S(2)}) collective-permute-start(bf16[8,32,256]{2,1,0:T(8,128)(2,1)S(1)} %all_gather.15), channel_id=1, source_target_pairs={{0,4},{4,8},{8,12},{12,16},{16,20},{20,24},{24,28},{28,32},{32,36}... | collective-permute-start | bytes 393224 | tf_op jit(solution)/shard_map/ppermute | solution.py:16
  248.4 1.9 copy-start.1
Sparse Core Ops, SparseCore 0:
  10.1 38.1 all-gather.1
where the time goes:
time: 258 us; the launch traced here: 257 us
  blocking collectives  76.4 us (30%)
  waiting for transfers between devices  71.2 us (28%)
  starting transfers between devices  35.4 us (14%)
  local copies, waits for them, and re-layouts  33.3 us (13%)
  matrix products  16.3 us (6%)
  between operations  14.1 us (5%)
  other arithmetic  10.4 us (4%)
    all_gather x3, blocking collectives, neighbour_rows(): slab_rows = lax.all_gather(vec_rounded, 'col', axis=0, tiled=True)  76.4 us
    all_gather x1, waiting for transfers between devices, per_device(): wide_basis = lax.all_gather(basis, 'col', axis=0, tiled=True)  40.4 us
    ppermute x4, starting transfers between devices, with_halo(): lax.ppermute(head, axis, [((i + 1) % count, i) for i in range(count)])  24.7 us
    ppermute x4, waiting for transfers between devices, with_halo(): lax.ppermute(tail, axis, [(i, (i + 1) % count) for i in range(count)])  24.1 us
    convert_element_type x1, local copies, waits for them, and re-layouts, per_device(): coarse_tiles[:, 0].astype(jnp.float32)  17.5 us
    ppermute x4, starting transfers between devices, with_halo(): lax.ppermute(tail, axis, [(i, (i + 1) % count) for i in range(count)])  10.7 us
    concatenate x4, other arithmetic, with_halo(): jnp.concatenate([lax.ppermute(tail, axis, [(i, (i + 1) % count) for i in...  7.86 us
    ppermute x4, waiting for transfers between devices, with_halo(): lax.ppermute(head, axis, [((i + 1) % count, i) for i in range(count)])  6.03 us
  transfers between devices with their start and end apart: 9, of which 7 were waited for; matrix products, arithmetic and copies ran while one was open for 5% of the time, Pallas kernels for 0%

commit v1 on v0

--- a/solution.py
+++ b/solution.py
@@ -52,7 +52,9 @@
     x_first = smooth(rhs)
     x_second = x_first + smooth(rhs - fine_apply(x_first))
     fine_residual = rhs - fine_apply(x_second)
-    wide_basis = lax.all_gather(basis, "col", axis=0, tiled=True)
+    wide_basis = jnp.concatenate(
+        lax.all_to_all(jnp.stack([basis] * lax.axis_size("col")), "col", 0, 0), axis=0
+    )
     near_basis = with_halo(wide_basis, (("slab", 0),), wide_basis.shape[0])
     picked_basis = jnp.take(near_basis, row_place, axis=0)
     upper = jnp.einsum(

time: 258 us -> 235 us (0.911)
  waiting for transfers between devices: 71.2 us -> 30.7 us
  blocking collectives: 76.4 us -> 101 us
  between operations: 14.1 us -> 0.8 us
  starting transfers between devices: 35.4 us -> 41.4 us
    all_gather x1 -> x0, waiting for transfers between devices: 40.4 us -> none  [per_device(): wide_basis = lax.all_gather(basis, 'col', axis=0, tiled=True)]
    all_to_all x0 -> x1, blocking collectives: none -> 29.2 us  [per_device(): lax.all_to_all(jnp.stack([basis] * lax.axis_size('col')), 'col', 0, 0)]
    ppermute x4, starting transfers between devices: 24.7 us -> 30.5 us  [with_halo(): lax.ppermute(head, axis, [((i + 1) % count, i) for i in range(count)])]
    all_gather x3, blocking collectives: 76.4 us -> 72 us  [neighbour_rows(): slab_rows = lax.all_gather(vec_rounded, 'col', axis=0, tiled=True)]
  transfers between devices with their start and end apart: 9 -> 8, of which waited for: 7 -> 6; matrix products, arithmetic and copies ran while one was open for 5% -> 5% of each run, Pallas kernels for 0% -> 0%
where the time goes in v1:
time: 235 us; the launch traced here: 233 us
  blocking collectives  101 us (43%)
  starting transfers between devices  41.4 us (18%)
  local copies, waits for them, and re-layouts  34.6 us (15%)
  waiting for transfers between devices  30.7 us (13%)
  matrix products  15.2 us (6%)
  other arithmetic  9.68 us (4%)
    all_gather x3, blocking collectives, neighbour_rows(): slab_rows = lax.all_gather(vec_rounded, 'col', axis=0, tiled=True)  72 us
    ppermute x4, starting transfers between devices, with_halo(): lax.ppermute(head, axis, [((i + 1) % count, i) for i in range(count)])  30.5 us
    all_to_all x1, blocking collectives, per_device(): lax.all_to_all(jnp.stack([basis] * lax.axis_size('col')), 'col', 0, 0)  29.2 us
    ppermute x4, waiting for transfers between devices, with_halo(): lax.ppermute(tail, axis, [(i, (i + 1) % count) for i in range(count)])  24 us
    convert_element_type x1, local copies, waits for them, and re-layouts, per_device(): coarse_tiles[:, 0].astype(jnp.float32)  17.5 us
    ppermute x4, starting transfers between devices, with_halo(): lax.ppermute(tail, axis, [(i, (i + 1) % count) for i in range(count)])  10.9 us
    concatenate x4, other arithmetic, with_halo(): jnp.concatenate([lax.ppermute(tail, axis, [(i, (i + 1) % count) for i in...  7.86 us
    ppermute x4, waiting for transfers between devices, with_halo(): lax.ppermute(head, axis, [((i + 1) % count, i) for i in range(count)])  6.7 us
  transfers between devices with their start and end apart: 8, of which 6 were waited for; matrix products, arithmetic and copies ran while one was open for 5% of the time, Pallas kernels for 0%

profile of v1, /device:TPU:1, one launch (start us, length us, event | category | flops | bytes accessed | tf_op | source)
XLA Modules:
  0.0 233.5 jit_solution(5569991958105615460)
XLA Ops:
  0.6 0.0 copy-start
  0.6 0.0 copy-start.1
  0.7 0.0 copy-start.2
  0.7 1.3 stack.2
  2.0 0.0 copy-start.4
  2.0 29.2 %all_to_all.5 = bf16[4,2,256,384]{3,2,1,0:T(8,128)(2,1)} all-to-all(bf16[4,2,256,384]{3,2,1,0:T(8,128)(2,1)S(1)} %stack.2), channel_id=1, replica_groups=mesh['slab'=128,'col'=4] {'col'}, dimensions={0} | all-to-all | bytes 3145728 | tf_op jit(solution)/shard_map/all_to_all | solution.py:56
  31.1 10.6 %collective-permute-start.5 = (bf16[8,256,384]{2,1,0:T(8,128)(2,1)}, bf16[8,256,384]{2,1,0:T(8,128)(2,1)}, u32[]{:S(2)}, u32[]{:S(2)}) collective-permute-start(bf16[8,256,384]{2,1,0:T(8,128)(2,1)} %bitcast.6), channel_id=1, source_target_pairs={{4,0},{8,4},{12,8},{16,12},{20,16},{24,20},{28,24},{32,28},{36,32}... | collective-permute-start | bytes 4718600 | tf_op jit(solution)/shard_map/ppermute | solution.py:18
  41.7 1.9 collective-permute-start.4
  43.7 0.0 copy-done.1
  43.7 0.0 copy-done.2
  43.7 0.8 fusion.56
  44.5 58.3 %all_gather.9 = bf16[8,32,384]{2,1,0:T(8,128)(2,1)} all-gather(bf16[2,32,384]{2,1,0:T(8,128)(2,1)S(1)} %get-tuple-element.5), channel_id=1, replica_groups=mesh['slab'=128,'col'=4] {'col'}, dimensions={0}, use_global_device_ids=true | all-gather | bytes 245760 | tf_op jit(solution)/shard_map/all_gather | solution.py:26
  102.8 13.4 %collective-permute-start.1 = (bf16[8,32,384]{2,1,0:T(8,128)(2,1)}, bf16[8,32,384]{2,1,0:T(8,128)(2,1)}, u32[]{:S(2)}, u32[]{:S(2)}) collective-permute-start(bf16[8,32,384]{2,1,0:T(8,128)(2,1)} %all_gather.9), channel_id=1, source_target_pairs={{4,0},{8,4},{12,8},{16,12},{20,16},{24,20},{28,24},{32,28},{36,32}... | collective-permute-start | bytes 589832 | tf_op jit(solution)/shard_map/ppermute | solution.py:18
  116.2 1.9 collective-permute-start
  118.2 0.0 copy-done.4
  118.2 0.1 reshape.70
  118.3 2.3 collective-permute-done.1
  120.6 9.6 %collective-permute-done = bf16[8,32,384]{2,1,0:T(8,128)(2,1)} collective-permute-done((bf16[8,32,384]{2,1,0:T(8,128)(2,1)}, bf16[8,32,384]{2,1,0:T(8,128)(2,1)}, u32[]{:S(2)}, u32[]{:S(2)}) %collective-permute-start) | collective-permute-done | bytes 196640 | tf_op jit(solution)/shard_map/ppermute | solution.py:16
  130.2 2.0 pad_maximum_fusion.1
  132.2 2.4 %gather_fusion.3 = bf16[12,32,384]{2,1,0:T(8,128)(2,1)} fusion(bf16[24,32,384]{2,1,0:T(8,128)(2,1)} %pad_maximum_fusion.1, s32[1024]{0:T(1024)S(1)} %pad_clamp_fusion), kind=kCustom, calls=%fused_computation.clone | custom fusion | bytes 589872 | tf_op jit(solution)/shard_map/jit(_take)/gather | solution.py:49
  134.6 0.0 copy-done
  134.6 2.7 %fusion.57 = (bf16[2,32,384]{2,1,0:T(8,128)(2,1)}, f32[2,32,384]{2,1,0:T(8,128)}) fusion(f32[2,32,384]{2,1,0:T(8,128)} %get-tuple-element.6, bf16[2,384,384]{2,1,0:T(8,128)(2,1)} %param.10, f32[2,32,384]{2,1,0:T(8,128)} %param.7, bf16[2,6,384,384]{3,2,1,0:T(8,128)(2,1)S(1)} %copy-done, bf16[2,6,32,384]{3,2,1,0:T(8,128)(2,1)} %bitcast.61, ...), kind=kOutput, calls=%fused_computation.67 | convolution fusion | flops 132366336 | bytes 4767756 | tf_op jit(solution)/shard_map/gri,gio->gro/dot_general | solution.py:40
  137.3 6.9 %all_gather.10 = bf16[8,32,384]{2,1,0:T(8,128)(2,1)S(1)} all-gather(bf16[2,32,384]{2,1,0:T(8,128)(2,1)} %get-tuple-element.7), channel_id=1, replica_groups=mesh['slab'=128,'col'=4] {'col'}, dimensions={0}, use_global_device_ids=true | all-gather | bytes 245760 | tf_op jit(solution)/shard_map/all_gather | solution.py:26
  144.2 4.2 %collective-permute-start.3 = (bf16[8,32,384]{2,1,0:T(8,128)(2,1)S(1)}, bf16[8,32,384]{2,1,0:T(8,128)(2,1)S(1)}, u32[]{:S(2)}, u32[]{:S(2)}) collective-permute-start(bf16[8,32,384]{2,1,0:T(8,128)(2,1)S(1)} %all_gather.10), channel_id=1, source_target_pairs={{4,0},{8,4},{12,8},{16,12},{20,16},{24,20},{28,24},{32,28},{36,32}... | collective-permute-start | bytes 589832 | tf_op jit(solution)/shard_map/ppermute | solution.py:18
  148.4 2.6 %collective-permute-start.2 = (bf16[8,32,384]{2,1,0:T(8,128)(2,1)S(1)}, bf16[8,32,384]{2,1,0:T(8,128)(2,1)S(1)}, u32[]{:S(2)}, u32[]{:S(2)}) collective-permute-start(bf16[8,32,384]{2,1,0:T(8,128)(2,1)S(1)} %all_gather.10), channel_id=1, source_target_pairs={{0,4},{4,8},{8,12},{12,16},{16,20},{20,24},{24,28},{28,32},{32,36}... | collective-permute-start | bytes 589832 | tf_op jit(solution)/shard_map/ppermute | solution.py:16
  151.0 2.9 %collective-permute-done.3 = bf16[8,32,384]{2,1,0:T(8,128)(2,1)S(1)} collective-permute-done((bf16[8,32,384]{2,1,0:T(8,128)(2,1)S(1)}, bf16[8,32,384]{2,1,0:T(8,128)(2,1)S(1)}, u32[]{:S(2)}, u32[]{:S(2)}) %collective-permute-start.3) | collective-permute-done | bytes 196640 | tf_op jit(solution)/shard_map/ppermute | solution.py:18
  153.9 8.2 %collective-permute-done.2 = bf16[8,32,384]{2,1,0:T(8,128)(2,1)S(1)} collective-permute-done((bf16[8,32,384]{2,1,0:T(8,128)(2,1)S(1)}, bf16[8,32,384]{2,1,0:T(8,128)(2,1)S(1)}, u32[]{:S(2)}, u32[]{:S(2)}) %collective-permute-start.2) | collective-permute-done | bytes 196640 | tf_op jit(solution)/shard_map/ppermute | solution.py:16
  162.1 0.9 pad_maximum_fusion.2
  163.0 2.4 %gather_fusion.4 = bf16[12,32,384]{2,1,0:T(8,128)(2,1)} fusion(bf16[24,32,384]{2,1,0:T(8,128)(2,1)} %pad_maximum_fusion.2, s32[1024]{0:T(1024)S(1)} %pad_clamp_fusion), kind=kCustom, calls=%fused_computation.1.clone | custom fusion | bytes 589872 | tf_op jit(solution)/shard_map/jit(_take)/gather | solution.py:49
  165.3 0.0 collective-permute-done.5
  165.3 0.0 collective-permute-done.4
  165.3 4.2 %pad_maximum_fusion = bf16[24,256,384]{2,1,0:T(8,128)(2,1)} fusion(bf16[8,256,384]{2,1,0:T(8,128)(2,1)} %collective-permute-done.5, bf16[8,256,384]{2,1,0:T(8,128)(2,1)} %bitcast.6, bf16[8,256,384]{2,1,0:T(8,128)(2,1)} %collective-permute-done.4), kind=kLoop, calls=%fused_computation.5 | loop fusion | flops 4718592 | bytes 9437184 | tf_op jit(solution)/shard_map/concatenate | solution.py:14
  169.5 4.8 %gather_fusion = bf16[12,256,384]{2,1,0:T(8,128)(2,1)} fusion(bf16[24,256,384]{2,1,0:T(8,128)(2,1)} %pad_maximum_fusion, s32[1024]{0:T(1024)S(1)} %pad_clamp_fusion), kind=kCustom, calls=%fused_computation.2 | custom fusion | bytes 4718640 | tf_op jit(solution)/shard_map/jit(_take)/gather | solution.py:59
  174.3 5.3 %fusion.9 = bf16[2,6,256,256]{3,2,1,0:T(8,128)(2,1)} fusion(bf16[2,6,384,384]{3,2,1,0:T(8,128)(2,1)S(1)} %copy-done, bf16[2,6,256,384]{3,2,1,0:T(8,128)(2,1)} %bitcast.59, pred[2,6]{1,0:T(4,128)(4,1)S(1)} %get-tuple-element.3, bf16[2,256,384]{2,1,0:T(8,128)(2,1)} %param.11), kind=kOutput, calls=%fused_computation.11 | convolution fusion | flops 1513095168 | bytes 7864332 | tf_op jit(solution)/shard_map/gtco,gdo->gtcd/dot_general | solution.py:63
  179.6 1.8 fusion.34
  181.4 17.5 %copy.11 = f32[2,256,256]{0,2,1:T(8,128)} copy(f32[2,256,256]{2,1,0:T(8,128)} %fusion.34) | data formatting | bytes 1048576 | tf_op jit(solution)/shard_map/convert_element_type | solution.py:66
  198.9 3.0 %gather_fusion.1 = f32[256,2]{1,0:T(8,128)} fusion(f32[2,256,256]{0,2,1:T(8,128)} %copy.11, s32[256]{0:T(256)S(1)} %bitcast.58), kind=kCustom, calls=%fused_computation.3 | custom fusion | bytes 6144 | tf_op jit(solution)/shard_map/jit(diagonal)/gather | solution.py:66
  201.8 1.0 copy.12
  202.8 2.6 %fusion.42 = (bf16[2,32,256]{2,1,0:T(8,128)(2,1)}, f32[2,32,256]{2,1,0:T(8,128)}) fusion(f32[2,256]{1,0:T(2,128)S(1)} %copy.12, bf16[2,256,384]{2,1,0:T(8,128)(2,1)} %param.11, f32[2,32,384]{2,1,0:T(8,128)} %param.7, bf16[2,6,384,384]{3,2,1,0:T(8,128)(2,1)S(1)} %copy-done, bf16[2,6,32,384]{3,2,1,0:T(8,128)(2,1)} %bitcast.60, ...), kind=kOutput, calls=%fused_computation.43 | convolution fusion | flops 126074880 | bytes 4425740 | tf_op jit(solution)/shard_map/gri,gci->grc/dot_general | solution.py:67
  205.4 6.8 %all_gather.11 = bf16[8,32,256]{2,1,0:T(8,128)(2,1)S(1)} all-gather(bf16[2,32,256]{2,1,0:T(8,128)(2,1)} %get-tuple-element.9), channel_id=1, replica_groups=mesh['slab'=128,'col'=4] {'col'}, dimensions={0}, use_global_device_ids=true | all-gather | bytes 163840 | tf_op jit(solution)/shard_map/all_gather | solution.py:26
  212.2 2.3 collective-permute-start.7
  214.5 4.5 %collective-permute-start.6 = (bf16[8,32,256]{2,1,0:T(8,128)(2,1)S(1)}, bf16[8,32,256]{2,1,0:T(8,128)(2,1)S(1)}, u32[]{:S(2)}, u32[]{:S(2)}) collective-permute-start(bf16[8,32,256]{2,1,0:T(8,128)(2,1)S(1)} %all_gather.11), channel_id=1, source_target_pairs={{0,4},{4,8},{8,12},{12,16},{16,20},{20,24},{24,28},{28,32},{32,36}... | collective-permute-start | bytes 393224 | tf_op jit(solution)/shard_map/ppermute | solution.py:16
  219.0 1.5 collective-permute-done.7
  220.5 6.2 %collective-permute-done.6 = bf16[8,32,256]{2,1,0:T(8,128)(2,1)S(1)} collective-permute-done((bf16[8,32,256]{2,1,0:T(8,128)(2,1)S(1)}, bf16[8,32,256]{2,1,0:T(8,128)(2,1)S(1)}, u32[]{:S(2)}, u32[]{:S(2)}) %collective-permute-start.6) | collective-permute-done | bytes 131104 | tf_op jit(solution)/shard_map/ppermute | solution.py:16
  226.7 0.8 pad_maximum_fusion.3
  227.5 2.2 gather_fusion.2
  229.8 1.8 fusion.23
  231.6 0.0 copy-start.3
  231.6 1.9 convolution_add_fusion.1
  233.5 0.0 copy-done.3
  (3 shorter events, 0.0 us)
Async XLA Ops:
  0.6 134.0 %copy-start = (bf16[2,6,384,384]{3,2,1,0:T(8,128)(2,1)S(1)}, bf16[2,6,384,384]{3,2,1,0:T(8,128)(2,1)}, u32[]{:S(2)}) copy-start(bf16[2,6,384,384]{3,2,1,0:T(8,128)(2,1)} %param.8) | copy-start | bytes 10616836
  0.6 43.0 %copy-start.1 = (bf16[2,384,384]{2,1,0:T(8,128)(2,1)S(1)}, bf16[2,384,384]{2,1,0:T(8,128)(2,1)}, u32[]{:S(2)}) copy-start(bf16[2,384,384]{2,1,0:T(8,128)(2,1)} %param.10) | copy-start | bytes 1769476
  0.7 43.0 %copy-start.2 = (f32[2,32,384]{2,1,0:T(8,128)S(1)}, f32[2,32,384]{2,1,0:T(8,128)}, u32[]{:S(2)}) copy-start(f32[2,32,384]{2,1,0:T(8,128)} %param.7) | copy-start | bytes 294916
  2.0 116.2 %copy-start.4 = (s32[2,6]{1,0:T(2,128)S(1)}, s32[2,6]{1,0:T(2,128)}, u32[]{:S(2)}) copy-start(s32[2,6]{1,0:T(2,128)} %param.9) | copy-start | bytes 148
  31.1 134.2 %collective-permute-start.5 = (bf16[8,256,384]{2,1,0:T(8,128)(2,1)}, bf16[8,256,384]{2,1,0:T(8,128)(2,1)}, u32[]{:S(2)}, u32[]{:S(2)}) collective-permute-start(bf16[8,256,384]{2,1,0:T(8,128)(2,1)} %bitcast.6), channel_id=1, source_target_pairs={{4,0},{8,4},{12,8},{16,12},{20,16},{24,20},{28,24},{32,28},{36,32}... | collective-permute-start | bytes 4718600 | tf_op jit(solution)/shard_map/ppermute | solution.py:18
  41.7 123.6 %collective-permute-start.4 = (bf16[8,256,384]{2,1,0:T(8,128)(2,1)}, bf16[8,256,384]{2,1,0:T(8,128)(2,1)}, u32[]{:S(2)}, u32[]{:S(2)}) collective-permute-start(bf16[8,256,384]{2,1,0:T(8,128)(2,1)} %bitcast.6), channel_id=1, source_target_pairs={{0,4},{4,8},{8,12},{12,16},{16,20},{20,24},{24,28},{28,32},{32,36}... | collective-permute-start | bytes 4718600 | tf_op jit(solution)/shard_map/ppermute | solution.py:16
  102.8 17.8 %collective-permute-start.1 = (bf16[8,32,384]{2,1,0:T(8,128)(2,1)}, bf16[8,32,384]{2,1,0:T(8,128)(2,1)}, u32[]{:S(2)}, u32[]{:S(2)}) collective-permute-start(bf16[8,32,384]{2,1,0:T(8,128)(2,1)} %all_gather.9), channel_id=1, source_target_pairs={{4,0},{8,4},{12,8},{16,12},{20,16},{24,20},{28,24},{32,28},{36,32}... | collective-permute-start | bytes 589832 | tf_op jit(solution)/shard_map/ppermute | solution.py:18
  116.2 14.0 %collective-permute-start = (bf16[8,32,384]{2,1,0:T(8,128)(2,1)}, bf16[8,32,384]{2,1,0:T(8,128)(2,1)}, u32[]{:S(2)}, u32[]{:S(2)}) collective-permute-start(bf16[8,32,384]{2,1,0:T(8,128)(2,1)} %all_gather.9), channel_id=1, source_target_pairs={{0,4},{4,8},{8,12},{12,16},{16,20},{20,24},{24,28},{28,32},{32,36}... | collective-permute-start | bytes 589832 | tf_op jit(solution)/shard_map/ppermute | solution.py:16
  144.2 9.7 %collective-permute-start.3 = (bf16[8,32,384]{2,1,0:T(8,128)(2,1)S(1)}, bf16[8,32,384]{2,1,0:T(8,128)(2,1)S(1)}, u32[]{:S(2)}, u32[]{:S(2)}) collective-permute-start(bf16[8,32,384]{2,1,0:T(8,128)(2,1)S(1)} %all_gather.10), channel_id=1, source_target_pairs={{4,0},{8,4},{12,8},{16,12},{20,16},{24,20},{28,24},{32,28},{36,32}... | collective-permute-start | bytes 589832 | tf_op jit(solution)/shard_map/ppermute | solution.py:18
  148.4 13.6 %collective-permute-start.2 = (bf16[8,32,384]{2,1,0:T(8,128)(2,1)S(1)}, bf16[8,32,384]{2,1,0:T(8,128)(2,1)S(1)}, u32[]{:S(2)}, u32[]{:S(2)}) collective-permute-start(bf16[8,32,384]{2,1,0:T(8,128)(2,1)S(1)} %all_gather.10), channel_id=1, source_target_pairs={{0,4},{4,8},{8,12},{12,16},{16,20},{20,24},{24,28},{28,32},{32,36}... | collective-permute-start | bytes 589832 | tf_op jit(solution)/shard_map/ppermute | solution.py:16
  212.2 8.3 %collective-permute-start.7 = (bf16[8,32,256]{2,1,0:T(8,128)(2,1)S(1)}, bf16[8,32,256]{2,1,0:T(8,128)(2,1)S(1)}, u32[]{:S(2)}, u32[]{:S(2)}) collective-permute-start(bf16[8,32,256]{2,1,0:T(8,128)(2,1)S(1)} %all_gather.11), channel_id=1, source_target_pairs={{4,0},{8,4},{12,8},{16,12},{20,16},{24,20},{28,24},{32,28},{36,32}... | collective-permute-start | bytes 393224 | tf_op jit(solution)/shard_map/ppermute | solution.py:18
  214.5 12.2 %collective-permute-start.6 = (bf16[8,32,256]{2,1,0:T(8,128)(2,1)S(1)}, bf16[8,32,256]{2,1,0:T(8,128)(2,1)S(1)}, u32[]{:S(2)}, u32[]{:S(2)}) collective-permute-start(bf16[8,32,256]{2,1,0:T(8,128)(2,1)S(1)} %all_gather.11), channel_id=1, source_target_pairs={{0,4},{4,8},{8,12},{12,16},{16,20},{20,24},{24,28},{28,32},{32,36}... | collective-permute-start | bytes 393224 | tf_op jit(solution)/shard_map/ppermute | solution.py:16
  231.6 1.9 copy-start.3
